TPU v7x, 128 devices: a whole 4x4x4 slice. The times are simulated.
128 devices in a mesh: req: 32 (over x, z, core), head: 4 (over y).
Axes of the slice: x: 4, y: 4, z: 4, core: 2. Of those that a mesh axis runs over, the one named last changes fastest.
Arguments:
- streams: bfloat16 [128, 64, 4, 2048], P('req'), may hold values from -6 to 6
- w_query: bfloat16 [2048, 2048], P(None, 'head'), may hold values from -0.125 to 0.125
- w_key: bfloat16 [2048, 2048], P(None, 'head'), may hold values from -0.125 to 0.125
- w_value: bfloat16 [2048, 2048], P(None, 'head'), may hold values from -0.125 to 0.125
- w_output: bfloat16 [2048, 2048], P('head'), may hold values from -0.125 to 0.125
- w_gate: bfloat16 [2048, 8192], P(None, 'req'), may hold values from -0.125 to 0.125
- w_up: bfloat16 [2048, 8192], P(None, 'req'), may hold values from -0.125 to 0.125
- w_down: bfloat16 [8192, 2048], P('req'), may hold values from -0.0625 to 0.0625
- cache_keys: bfloat16 [128, 1024, 2048], P('req', None, 'head'), may hold values from -250 to 250
- cache_values: bfloat16 [128, 1024, 2048], P('req', None, 'head'), may hold values from -6 to 6
- hc_in: float32 [2, 4], replicated, may hold values from 0.1 to 0.6
- hc_res: float32 [2, 4, 4], replicated, may hold values from -0.4 to 0.8
- hc_out: float32 [2, 4], replicated, may hold values from 0.5 to 1.5
- parents: int32 [128, 64], replicated, may hold values from 0 to 62, as said below
- draft_len: int32 [128], replicated, may hold values from 1 to 64, 6144 in all
- cache_len: int32 [128], replicated, may hold values from 1 to 1024, 65536 in all
- accept_pick: int32 [128], replicated, may hold values from 0 to 63
- slot_owner: int32 [128], replicated, may hold values from 0 to 127, each once
Outputs:
- new_streams: bfloat16 [128, 64, 4, 2048], P('req', 'head')
- accepted_kv: bfloat16 [128, 64, 2, 2048], P('req', None, None, 'head')
Inputs may be any that keep to these rules, and one draw needn't show every extreme that they name: parents[r, 0] = 0 and 0 <= parents[r, p] < p for p >= 1. `draft_len`: the live draft nodes of all requests sum to exactly 6144.
All inputs are finite; a program needn't handle non-finite values.
Results may differ from a plain program's by a relative error of at most 0.024.
Values may be sent and summed in bfloat16 or wider, within the bound.
No kernel may reach another device: no remote copies, remote signals or barrier semaphores. Data moves between devices by JAX's collectives and lax.ppermute only.
A program may use at most 128 MiB of HBM per device.

v0:
```python
import jax
import jax.numpy as jnp
from jax import lax
from jax.sharding import PartitionSpec as P

HD = 128


def ancestry(parent_ids):
    count = parent_ids.shape[-1]
    nodes = jnp.arange(count, dtype=jnp.int32)
    links = (parent_ids[..., :, None] == nodes).astype(jnp.float32)
    unit = (nodes[:, None] == nodes[None, :]).astype(jnp.float32)
    above = jnp.minimum(links + unit, 1.0)
    for rounds in range((count - 1).bit_length()):
        above = jnp.minimum(jnp.matmul(above, above, precision=lax.Precision.HIGHEST), 1.0)
    depth = jnp.sum(above, axis=-1) - 1.0
    return (above, depth)


def normalize(values):
    center = jnp.mean(values, axis=-1, keepdims=True)
    spread = jnp.mean(jnp.square(values - center), axis=-1, keepdims=True)
    return (values - center) * lax.rsqrt(spread + 1e-05)


def rotate(values, position, head_size):
    half = head_size // 2
    freq = jnp.power(10000.0, -(jnp.arange(half, dtype=jnp.float32) * 2.0 / head_size))
    angle = position[..., None] * freq
    shaped = values.reshape(values.shape[:-1] + (-1, head_size))
    first, second = (shaped[..., :half], shaped[..., half:])
    cosine = jnp.cos(angle)[..., None, :]
    sine = jnp.sin(angle)[..., None, :]
    turned = jnp.concatenate(
        [first * cosine - second * sine, second * cosine + first * sine], axis=-1
    )
    return turned.reshape(values.shape)


def body(
    streams,
    w_query,
    w_key,
    w_value,
    w_output,
    w_gate,
    w_up,
    w_down,
    cache_keys,
    cache_values,
    hc_in,
    hc_res,
    hc_out,
    parents,
    draft_len,
    cache_len,
    accept_pick,
    slot_owner,
):
    highest = lax.Precision.HIGHEST
    local_slots, draft, stream_count, width = streams.shape
    local_width = w_query.shape[1]
    local_heads = local_width // HD
    cache_size = cache_keys.shape[1]
    groups = lax.axis_size("head")
    quarter = draft // groups
    requests = slot_owner.shape[0]
    scale = HD ** (-0.5)
    req_index = lax.axis_index("req")
    everyone = jnp.arange(requests, dtype=jnp.int32)
    my_slots = req_index * local_slots + jnp.arange(local_slots, dtype=jnp.int32)
    slot_pick = everyone[None, :] == my_slots[:, None]
    owner = jnp.sum(jnp.where(slot_pick, slot_owner[None, :], 0), axis=1)
    owner_pick = everyone[None, :] == owner[:, None]

    def lookup(table):
        return jnp.sum(jnp.where(owner_pick, table[None, :], 0), axis=1)

    parent_ids = jnp.sum(jnp.where(owner_pick[:, :, None], parents[None, :, :], 0), axis=1)
    draft_count = lookup(draft_len)
    cache_count = lookup(cache_len)
    accepted = jnp.minimum(lookup(accept_pick), draft_count - 1)
    above, depth = ancestry(parent_ids)
    hidden = streams.astype(jnp.float32)
    mixed_in = jnp.einsum("spmd,m->spd", hidden, hc_in[0], precision=highest)
    normed = normalize(mixed_in).astype(jnp.bfloat16).reshape(local_slots * draft, width)
    position = (cache_count.astype(jnp.float32)[:, None] + depth).reshape(-1)
    query = rotate(
        jnp.dot(normed, w_query, preferred_element_type=jnp.float32), position, HD
    ).astype(jnp.bfloat16)
    keys = rotate(jnp.dot(normed, w_key, preferred_element_type=jnp.float32), position, HD).astype(
        jnp.bfloat16
    )
    values = jnp.dot(normed, w_value, preferred_element_type=jnp.float32).astype(jnp.bfloat16)
    query_h = query.reshape(local_slots, draft, local_heads, HD)
    keys_h = keys.reshape(local_slots, draft, local_heads, HD)
    values_h = values.reshape(local_slots, draft, local_heads, HD)
    stored_keys = cache_keys.reshape(local_slots, cache_size, local_heads, HD)
    stored_values = cache_values.reshape(local_slots, cache_size, local_heads, HD)
    cached = (
        jnp.einsum("sphe,sche->shpc", query_h, stored_keys, preferred_element_type=jnp.float32)
        * scale
    )
    live = jnp.arange(cache_size, dtype=jnp.int32)[None, :] < cache_count[:, None]
    cached = jnp.where(live[:, None, None, :], cached, -1e30)
    local = (
        jnp.einsum("sphe,sqhe->shpq", query_h, keys_h, preferred_element_type=jnp.float32) * scale
    )
    local = jnp.where((above > 0.5)[:, None, :, :], local, -1e30)
    top = jnp.maximum(jnp.max(cached, axis=-1), jnp.max(local, axis=-1))[..., None]
    cached_exp = jnp.exp(cached - top)
    local_exp = jnp.exp(local - top)
    total = jnp.sum(cached_exp, axis=-1, keepdims=True) + jnp.sum(local_exp, axis=-1, keepdims=True)
    weight_cache = (cached_exp / total).astype(jnp.bfloat16)
    weight_local = (local_exp / total).astype(jnp.bfloat16)
    attended = jnp.einsum(
        "shpc,sche->pshe", weight_cache, stored_values, preferred_element_type=jnp.float32
    )
    attended = attended + jnp.einsum(
        "shpq,sqhe->pshe", weight_local, values_h, preferred_element_type=jnp.float32
    )
    attended = attended.astype(jnp.bfloat16).reshape(draft, local_slots, local_width)
    attn_out = lax.psum_scatter(
        jnp.einsum("psk,kd->psd", attended, w_output, preferred_element_type=jnp.float32).astype(
            jnp.bfloat16
        ),
        "head",
        scatter_dimension=0,
        tiled=True,
    ).astype(jnp.float32)
    head_index = lax.axis_index("head")
    first_position = head_index * quarter
    own = lax.dynamic_slice_in_dim(hidden, first_position, quarter, 1)
    carried = jnp.einsum("spnd,nm->spmd", own, hc_res[0], precision=highest)
    carried = (
        carried + hc_out[0][None, None, :, None] * jnp.transpose(attn_out, (1, 0, 2))[:, :, None, :]
    )
    own_rows = local_slots * quarter
    first = carried.astype(jnp.bfloat16).reshape(own_rows, stream_count, width)
    positions_here = first_position + jnp.arange(quarter, dtype=jnp.int32)
    valid = (positions_here[None, :] < draft_count[:, None]).reshape(-1)
    rows_wide = first.astype(jnp.float32)
    normed_rows = normalize(jnp.einsum("nmd,m->nd", rows_wide, hc_in[1], precision=highest)).astype(
        jnp.bfloat16
    )
    piece = lax.all_gather(normed_rows, "req", axis=0, tiled=True)
    gate = jnp.dot(piece, w_gate, preferred_element_type=jnp.float32)
    upward = jnp.dot(piece, w_up, preferred_element_type=jnp.float32)
    inner = (jax.nn.silu(gate) * upward).astype(jnp.bfloat16)
    mlp_out = lax.psum_scatter(
        jnp.dot(inner, w_down, preferred_element_type=jnp.float32).astype(jnp.bfloat16),
        "req",
        scatter_dimension=0,
        tiled=True,
    ).astype(jnp.float32)
    final_rows = jnp.einsum("nkd,km->nmd", rows_wide, hc_res[1], precision=highest)
    final = jnp.where(
        valid[:, None, None], final_rows + hc_out[1][None, :, None] * mlp_out[:, None, :], 0.0
    ).astype(jnp.bfloat16)
    new_streams = final.reshape(local_slots, quarter, stream_count, width)
    nodes = jnp.arange(draft, dtype=jnp.int32)
    path_row = jnp.sum(
        jnp.where((nodes[None, :] == accepted[:, None])[:, :, None], above, 0.0), axis=1
    )
    take = (
        (depth[:, None, :] == nodes.astype(jnp.float32)[None, :, None])
        & (path_row[:, None, :] > 0.5)
    ).astype(jnp.bfloat16)
    keys_rows = keys.reshape(local_slots, draft, local_width)
    values_rows = values.reshape(local_slots, draft, local_width)
    new_keys = jnp.einsum(
        "stq,sqk->stk", take, keys_rows, preferred_element_type=jnp.float32
    ).astype(jnp.bfloat16)
    new_values = jnp.einsum(
        "stq,sqk->stk", take, values_rows, preferred_element_type=jnp.float32
    ).astype(jnp.bfloat16)
    accepted_kv = jnp.stack([new_keys, new_values], axis=2)
    return (new_streams, accepted_kv)


def solution(mesh):
    placed = (
        P("req", None, None, None),
        P(None, "head"),
        P(None, "head"),
        P(None, "head"),
        P("head", None),
        P(None, "req"),
        P(None, "req"),
        P("req", None),
        P("req", None, "head"),
        P("req", None, "head"),
        P(),
        P(),
        P(),
        P(),
        P(),
        P(),
        P(),
        P(),
    )
    return jax.shard_map(
        body,
        mesh=mesh,
        in_specs=placed,
        out_specs=(P("req", "head", None, None), P("req", None, None, "head")),
        check_vma=False,
    )
```

profile of v0, /device:TPU:0, one launch (start us, length us, event | category | flops | bytes accessed | tf_op | source)
XLA Modules:
  0.0 265.1 jit_solution(14680197965514249326)
XLA Ops:
  7.8 0.9 select_reduce_fusion.5
  8.7 0.9 select_reduce_fusion.2
  9.8 0.9 select_reduce_fusion.1
  13.4 8.5 %fusion.58 = f32[1,4,64,2048]{3,0,2,1:T(1,128)S(1)} fusion(bf16[4,64,4,2048]{3,2,1,0:T(4,128)(2,1)} %param.18, f32[2,4]{1,0:T(2,128)S(1)} %copy-done.11), kind=kOutput, calls=%fused_computation.125 | convolution fusion | flops 25165824 | bytes 6291968 | tf_op jit(solution)/shard_map/spmd,m->spd/dot_general | solution.py:86
  23.2 0.7 multiply_convert_fusion
  24.0 0.8 copy-done.8
  24.8 0.7 convolution_convert_fusion.4
  25.5 0.8 reshape.273
  26.3 4.0 %copy.77 = bf16[512,2048]{1,0:T(8,128)(2,1)} copy(bf16[512,2048]{0,1:T(8,128)(2,1)} %bitcast.134) | data formatting | bytes 4194304 | tf_op jit(solution)/shard_map/dot_general | solution.py:90
  30.3 1.0 multiply_cosine_fusion
  31.3 2.3 fusion.65
  33.9 4.0 %copy.78 = bf16[512,2048]{1,0:T(8,128)(2,1)} copy(bf16[512,2048]{0,1:T(8,128)(2,1)} %bitcast.135) | data formatting | bytes 4194304 | tf_op jit(solution)/shard_map/dot_general | solution.py:92
  37.9 2.7 %fusion.66 = f32[256,4,128]{0,2,1:T(8,128)S(1)} fusion(bf16[256,2048,1]{1,0,2:T(8,128)(2,1)} %bitcast.142, bf16[4,128,2048]{2,1,0:T(8,128)(2,1)} %bitcast.137), kind=kOutput, calls=%fused_computation.134 | convolution fusion | flops 536870912 | bytes 3670016 | tf_op jit(solution)/shard_map/dot_general | solution.py:92
  40.7 0.8 copy.60
  41.5 1.2 fusion.64
  42.8 3.8 %fusion.6 = (f32[4,4,64]{2,1,0:T(4,128)S(1)}, f32[4,4,64,1024]{3,2,1,0:T(8,128)S(1)}) fusion(pred[4,1024]{1,0:T(4,128)(4,1)S(1)} %iota_compare_fusion.3, bf16[4,64,4,128]{3,1,0,2:T(8,128)(2,1)S(1)} %bitcast.139, bf16[4,1024,512]{2,1,0:T(8,128)(2,1)} %param.26), kind=kOutput, calls=%fused_computation.10 | convolution fusion | flops 271580160 | bytes 8658944 | tf_op jit(solution)/shard_map/sphe,sche->shpc/dot_general | solution.py:102
  46.7 1.1 fusion.7
  47.8 1.1 copy-done.7
  48.9 1.7 fusion.20
  50.9 1.7 convolution_convert_fusion.1
  52.7 26.1 %reduce-scatter.3.cloned.1.call-done = bf16[16,4,2048]{2,0,1:T(8,128)(2,1)} async-done(((bf16[64,4,2048]{2,0,1:T(8,128)(2,1)}), bf16[16,4,2048]{2,0,1:T(8,128)(2,1)}) %reduce-scatter.3.cloned.1.call-update) | async-done | bytes 262160 | tf_op jit(solution)/shard_map/reduce_scatter | solution.py:124
  78.8 1.0 convert_bitcast_fusion
  79.8 3.4 %fusion.11 = bf16[4,16,4,2048]{3,2,1,0:T(4,128)(2,1)S(1)} fusion(f32[4,16,2048]{2,1,0:T(8,128)S(1)} %convert_bitcast_fusion, f32[4]{0:T(128)S(1)} %get-tuple-element.22, bf16[4,64,4,2048]{3,2,1,0:T(4,128)(2,1)} %param.18, s32[]{:T(128)S(6)} %select_n.38, f32[2,4,4]{2,1,0:T(4,128)S(1)} %copy-done.10), kind=kOutput, calls=%fused_computation.18 | convolution fusion | flops 26738688 | bytes 2624004 | tf_op jit(solution)/shard_map/spnd,nm->spmd/dot_general | solution.py:135
  83.3 1.8 fusion.57
  85.6 0.9 multiply_convert_fusion.1
  86.6 52.8 %all-gather.2.cloned.1.call-done = bf16[2048,2048]{1,0:T(8,128)(2,1)} async-done(((bf16[64,2048]{1,0:T(8,128)(2,1)}), bf16[2048,2048]{1,0:T(8,128)(2,1)}) %all-gather.2.cloned.1.call-update) | async-done | bytes 8388624 | tf_op jit(solution)/shard_map/all_gather | solution.py:147
  139.3 7.1 %fusion.67 = f32[2048,256]{1,0:T(8,128)} fusion(bf16[2048,2048]{1,0:T(8,128)(2,1)} %all-gather.2.cloned.1.call-done, bf16[2048,256]{1,0:T(8,128)(2,1)S(1)} %copy-done.9), kind=kOutput, calls=%fused_computation.135 | convolution fusion | flops 2147483648 | bytes 11534336 | tf_op jit(solution)/shard_map/dot_general | solution.py:148
  146.4 13.8 %convolution_convert_fusion = bf16[2048,2048]{1,0:T(8,128)(2,1)} fusion(bf16[256,2048]{1,0:T(8,128)(2,1)} %param.25, bf16[2048,2048]{1,0:T(8,128)(2,1)} %all-gather.2.cloned.1.call-done, bf16[2048,256]{1,0:T(8,128)(2,1)} %param.24, f32[2048,256]{1,0:T(8,128)} %fusion.67), kind=kOutput, calls=%fused_computation | convolution fusion | flops 4302307328 | bytes 20971520 | tf_op jit(solution)/shard_map/dot_general | solution.py:152
  161.7 1.3 copy.69
  163.1 89.6 %reduce-scatter.5.cloned.1.call-done = bf16[64,2048]{1,0:T(8,128)(2,1)} async-done(((bf16[2048,2048]{1,0:T(8,128)(2,1)}), bf16[64,2048]{1,0:T(8,128)(2,1)}) %reduce-scatter.5.cloned.1.call-update) | async-done | bytes 262160 | tf_op jit(solution)/shard_map/reduce_scatter | solution.py:151
  252.7 1.0 convert_element_type.102
  253.7 4.9 %fusion.13 = bf16[64,4,2048]{2,1,0:T(4,128)(2,1)} fusion(bf16[64,4,2048]{2,1,0:T(4,128)(2,1)} %bitcast.146, f32[64,2048]{1,0:T(8,128)S(1)} %convert_element_type.102, f32[4]{0:T(128)S(1)} %get-tuple-element.21, pred[64]{0:T(512)(128)(4,1)S(1)} %lt.43, f32[2,4,4]{2,1,0:T(4,128)S(1)} %copy-done.10), kind=kOutput, calls=%fused_computation.21 | convolution fusion | flops 27262976 | bytes 2624512 | tf_op jit(solution)/shard_map/nkd,km->nmd/dot_general | solution.py:157
  (78 shorter events, 7.8 us)
Async XLA Ops:
  7.2 43.7 %copy-start = (bf16[512,2048]{1,0:T(8,128)(2,1)S(1)}, bf16[512,2048]{1,0:T(8,128)(2,1)}, u32[]{:S(2)}) copy-start(bf16[512,2048]{1,0:T(8,128)(2,1)} %param.22) | copy-start | bytes 6291460
  7.2 6.3 %copy-start.11 = (f32[2,4]{1,0:T(2,128)S(1)}, f32[2,4]{1,0:T(2,128)}, u32[]{:S(2)}) copy-start(f32[2,4]{1,0:T(2,128)} %param.28) | copy-start | bytes 100
  7.2 71.6 %reduce-scatter.3.cloned.1.call-start = ((), (), s32[]{:S(2)}) async-start(), calls=%async_computation.2 | async-start | bytes 1310720 | tf_op jit(solution)/shard_map/reduce_scatter | solution.py:124
  9.6 3.0 %copy-start.5 = (s32[4]{0:T(128)}, s32[4]{0:T(128)S(1)}, u32[]{:S(2)}) copy-start(s32[4]{0:T(128)S(1)} %get-tuple-element.11) | copy-start | bytes 52
  23.2 1.6 copy-start.8
  24.0 7.3 %copy-start.2 = (bf16[4,64,2048]{2,1,0:T(8,128)(2,1)}, bf16[4,64,2048]{2,1,0:T(8,128)(2,1)S(1)}, u32[]{:S(2)}) copy-start(bf16[4,64,2048]{2,1,0:T(8,128)(2,1)S(1)} %multiply_convert_fusion) | copy-start | bytes 3145732
  46.7 2.2 copy-start.7
  48.9 1.7 copy-start.3
  50.9 1.8 copy-start.4
  50.9 28.9 %copy-start.10 = (f32[2,4,4]{2,1,0:T(4,128)S(1)}, f32[2,4,4]{2,1,0:T(4,128)}, u32[]{:S(2)}) copy-start(f32[2,4,4]{2,1,0:T(4,128)} %param.29) | copy-start | bytes 388
  52.6 86.7 %all-gather.2.cloned.1.call-start = ((), (), s32[]{:S(2)}) async-start(), calls=%async_computation.3 | async-start | bytes 8650752 | tf_op jit(solution)/shard_map/all_gather | solution.py:147
  52.7 30.5 %copy-start.12 = (f32[2,4]{1,0:T(2,128)S(1)}, f32[2,4]{1,0:T(2,128)}, u32[]{:S(2)}) copy-start(f32[2,4]{1,0:T(2,128)} %param.28) | copy-start | bytes 100
  83.2 2.4 copy-start.13
  83.2 56.1 %copy-start.9 = (bf16[2048,256]{1,0:T(8,128)(2,1)S(1)}, bf16[2048,256]{1,0:T(8,128)(2,1)}, u32[]{:S(2)}) copy-start(bf16[2048,256]{1,0:T(8,128)(2,1)} %param.23) | copy-start | bytes 3145732
  86.5 166.1 %reduce-scatter.5.cloned.1.call-start = ((), (), s32[]{:S(2)}) async-start(), calls=%async_computation.4 | async-start | bytes 8650752 | tf_op jit(solution)/shard_map/reduce_scatter | solution.py:151
  160.2 0.6 copy-start.6
  253.7 5.0 %copy-start.1 = (bf16[512,2048]{1,0:T(8,128)(2,1)S(1)}, bf16[512,2048]{1,0:T(8,128)(2,1)}, u32[]{:S(2)}) copy-start(bf16[512,2048]{1,0:T(8,128)(2,1)} %param.22) | copy-start | bytes 6291460
Sparse Core Ops, SparseCore 0:
  52.8 26.0 reduce-scatter.2
  86.6 52.6 all-gather.1
  160.4 92.2 reduce-scatter.4
where the time goes:
time: 266 us; the launch traced here: 265 us
  waiting for transfers between devices  169 us (64%)
  matrix products  56.2 us (21%)
  local copies, waits for them, and re-layouts  14.7 us (6%)
  between operations  14.2 us (5%)
  other arithmetic  11.5 us (4%)
    reduce_scatter x1, waiting for transfers between devices, body(): lax.psum_scatter(jnp.dot(inner, w_down, preferred_element_type=jnp.float3...  89.6 us
    all_gather x1, waiting for transfers between devices, body(): piece = lax.all_gather(normed_rows, 'req', axis=0, tiled=True)  52.8 us
    reduce_scatter x1, waiting for transfers between devices, body(): lax.psum_scatter(jnp.einsum('psk,kd->psd', attended, w_output, preferred_...  26.1 us
    dot_general x1, matrix products, body(): jnp.dot(inner, w_down, preferred_element_type=jnp.float32)  13.8 us
    dot_general x1, matrix products, body(): mixed_in = jnp.einsum('spmd,m->spd', hidden, hc_in[0], precision=highest)  8.45 us
    dot_general x1, matrix products, body(): gate = jnp.dot(piece, w_gate, preferred_element_type=jnp.float32)  7.09 us
  transfers between devices with their start and end apart: 3, of which 3 were waited for; matrix products, arithmetic and copies ran while one was open for 1% of the time, Pallas kernels for 0%

commit v1 on v0

--- a/solution.py
+++ b/solution.py
@@ -4,6 +4,13 @@
 from jax.sharding import PartitionSpec as P
 
 HD = 128
+
+
+def all_by_exchange(x, mesh_axis, along):
+    size = lax.axis_size(mesh_axis)
+    blocks = jnp.stack([x for _ in range(size)])
+    blocks = lax.all_to_all(blocks, mesh_axis, split_axis=0, concat_axis=0)
+    return jnp.concatenate(blocks, axis=along)
 
 
 def ancestry(parent_ids):
@@ -144,7 +151,7 @@
     normed_rows = normalize(jnp.einsum("nmd,m->nd", rows_wide, hc_in[1], precision=highest)).astype(
         jnp.bfloat16
     )
-    piece = lax.all_gather(normed_rows, "req", axis=0, tiled=True)
+    piece = all_by_exchange(normed_rows, "req", 0)
     gate = jnp.dot(piece, w_gate, preferred_element_type=jnp.float32)
     upward = jnp.dot(piece, w_up, preferred_element_type=jnp.float32)
     inner = (jax.nn.silu(gate) * upward).astype(jnp.bfloat16)

time: 266 us -> 316 us (1.19)
  blocking collectives: 0 us -> 103 us
  waiting for transfers between devices: 169 us -> 113 us
  local copies, waits for them, and re-layouts: 14.7 us -> 18.9 us
    all_to_all x0 -> x1, blocking collectives: none -> 103 us  [all_by_exchange(): blocks = lax.all_to_all(blocks, mesh_axis, split_axis=0, concat_axis=0)]
    all_gather x1 -> x0, waiting for transfers between devices: 52.8 us -> none  [body(): piece = lax.all_gather(normed_rows, 'req', axis=0, tiled=True)]
    dot_general x1, matrix products: 7.09 us -> 3.79 us  [body(): gate = jnp.dot(piece, w_gate, preferred_element_type=jnp.float32)]
    unnamed x29 -> x33, local copies, waits for them, and re-layouts: 3.74 us -> 6.95 us
  transfers between devices with their start and end apart: 3 -> 2, of which waited for: 3 -> 2; matrix products, arithmetic and copies ran while one was open for 1% -> 1% of each run, Pallas kernels for 0% -> 0%
where the time goes in v1:
time: 316 us
  waiting for transfers between devices  113 us (36%)
  blocking collectives  103 us (33%)
  matrix products  56 us (18%)
  local copies, waits for them, and re-layouts  18.9 us (6%)
  between operations  14.5 us (5%)
  other arithmetic  10.8 us (3%)
    all_to_all x1, blocking collectives, all_by_exchange(): blocks = lax.all_to_all(blocks, mesh_axis, split_axis=0, concat_axis=0)  103 us
    reduce_scatter x1, waiting for transfers between devices, body(): lax.psum_scatter(jnp.dot(inner, w_down, preferred_element_type=jnp.float3...  86.7 us
    reduce_scatter x1, waiting for transfers between devices, body(): lax.psum_scatter(jnp.einsum('psk,kd->psd', attended, w_output, preferred_...  26.1 us
    dot_general x1, matrix products, body(): jnp.dot(inner, w_down, preferred_element_type=jnp.float32)  16.8 us
    dot_general x1, matrix products, body(): mixed_in = jnp.einsum('spmd,m->spd', hidden, hc_in[0], precision=highest)  8.45 us
    unnamed x33, local copies, waits for them, and re-layouts  6.95 us
  transfers between devices with their start and end apart: 2, of which 2 were waited for; matrix products, arithmetic and copies ran while one was open for 1% of the time, Pallas kernels for 0%

profile of v1, /device:TPU:0, one launch (start us, length us, event | category | flops | bytes accessed | tf_op | source)
XLA Modules:
  0.0 315.6 jit_solution(14907095489104090418)
XLA Ops:
  7.8 0.9 select_reduce_fusion.5
  8.7 0.9 select_reduce_fusion.2
  9.8 0.9 select_reduce_fusion.1
  13.4 8.5 %fusion.58 = f32[1,4,64,2048]{3,0,2,1:T(1,128)S(1)} fusion(bf16[4,64,4,2048]{3,2,1,0:T(4,128)(2,1)} %param.18, f32[2,4]{1,0:T(2,128)S(1)} %copy-done.13), kind=kOutput, calls=%fused_computation.125 | convolution fusion | flops 25165824 | bytes 6291968 | tf_op jit(solution)/shard_map/spmd,m->spd/dot_general | solution.py:93
  23.2 0.7 multiply_convert_fusion
  24.0 0.8 copy-done.9
  25.5 0.8 reshape.278
  26.3 4.0 %copy.77 = bf16[512,2048]{1,0:T(8,128)(2,1)} copy(bf16[512,2048]{0,1:T(8,128)(2,1)} %bitcast.137) | data formatting | bytes 4194304 | tf_op jit(solution)/shard_map/dot_general | solution.py:97
  30.3 1.0 multiply_cosine_fusion
  31.3 2.3 fusion.65
  33.9 4.0 %copy.78 = bf16[512,2048]{1,0:T(8,128)(2,1)} copy(bf16[512,2048]{0,1:T(8,128)(2,1)} %bitcast.138) | data formatting | bytes 4194304 | tf_op jit(solution)/shard_map/dot_general | solution.py:99
  37.9 2.7 fusion.66
  40.7 0.8 copy.60
  41.5 1.2 fusion.64
  42.8 3.8 %fusion.6 = (f32[4,4,64]{2,1,0:T(4,128)S(1)}, f32[4,4,64,1024]{3,2,1,0:T(8,128)S(1)}) fusion(pred[4,1024]{1,0:T(4,128)(4,1)S(1)} %iota_compare_fusion.3, bf16[4,64,4,128]{3,1,0,2:T(8,128)(2,1)S(1)} %bitcast.142, bf16[4,1024,512]{2,1,0:T(8,128)(2,1)} %param.26), kind=kOutput, calls=%fused_computation.10 | convolution fusion | flops 271580160 | bytes 8658944 | tf_op jit(solution)/shard_map/sphe,sche->shpc/dot_general | solution.py:109
  46.7 1.1 fusion.7
  47.8 1.1 copy-done.8
  48.9 1.7 fusion.20
  50.9 1.7 convolution_convert_fusion.1
  52.7 26.1 %reduce-scatter.3.cloned.1.call-done = bf16[16,4,2048]{2,0,1:T(8,128)(2,1)} async-done(((bf16[64,4,2048]{2,0,1:T(8,128)(2,1)}), bf16[16,4,2048]{2,0,1:T(8,128)(2,1)}) %reduce-scatter.3.cloned.1.call-update) | async-done | bytes 262160 | tf_op jit(solution)/shard_map/reduce_scatter | solution.py:131
  78.8 1.0 convert_bitcast_fusion
  79.8 3.4 %fusion.11 = bf16[4,16,4,2048]{3,2,1,0:T(4,128)(2,1)S(1)} fusion(f32[4,16,2048]{2,1,0:T(8,128)S(1)} %convert_bitcast_fusion, f32[4]{0:T(128)S(1)} %get-tuple-element.22, bf16[4,64,4,2048]{3,2,1,0:T(4,128)(2,1)} %param.18, s32[]{:T(128)S(6)} %select_n.38, f32[2,4,4]{2,1,0:T(4,128)S(1)} %copy-done.12), kind=kOutput, calls=%fused_computation.18 | convolution fusion | flops 26738688 | bytes 2624004 | tf_op jit(solution)/shard_map/spnd,nm->spmd/dot_general | solution.py:142
  83.3 1.8 fusion.57
  85.8 1.1 stack.8
  86.9 102.6 %all_to_all.5 = bf16[32,64,2048]{2,1,0:T(8,128)(2,1)S(1)} all-to-all(bf16[32,64,2048]{2,1,0:T(8,128)(2,1)S(1)} %stack.8), channel_id=1, replica_groups=mesh['req'=32,'head'=4] {'req'}, dimensions={0} | all-to-all | bytes 16777216 | tf_op jit(solution)/shard_map/all_to_all | solution.py:12
  189.4 3.2 %copy-done.2 = bf16[32,64,2048]{2,1,0:T(8,128)(2,1)} copy-done((bf16[32,64,2048]{2,1,0:T(8,128)(2,1)}, bf16[32,64,2048]{2,1,0:T(8,128)(2,1)S(1)}, u32[]{:S(2)}) %copy-start.2) | copy-done | bytes 8388632
  192.6 3.8 %fusion.67 = f32[2048,256]{1,0:T(8,128)} fusion(bf16[2048,2048]{1,0:T(8,128)(2,1)S(1)} %bitcast.135, bf16[2048,256]{1,0:T(8,128)(2,1)S(1)} %copy-done.10), kind=kOutput, calls=%fused_computation.135 | convolution fusion | flops 2147483648 | bytes 11534336 | tf_op jit(solution)/shard_map/dot_general | solution.py:155
  196.4 16.8 %convolution_convert_fusion = bf16[2048,2048]{1,0:T(8,128)(2,1)} fusion(bf16[256,2048]{1,0:T(8,128)(2,1)S(1)} %copy-done.11, bf16[2048,2048]{1,0:T(8,128)(2,1)} %bitcast.136, bf16[2048,256]{1,0:T(8,128)(2,1)} %param.24, f32[2048,256]{1,0:T(8,128)} %fusion.67), kind=kOutput, calls=%fused_computation | convolution fusion | flops 4302307328 | bytes 20971520 | tf_op jit(solution)/shard_map/dot_general | solution.py:159
  214.8 1.3 copy.69
  216.1 86.7 %reduce-scatter.5.cloned.1.call-done = bf16[64,2048]{1,0:T(8,128)(2,1)} async-done(((bf16[2048,2048]{1,0:T(8,128)(2,1)}), bf16[64,2048]{1,0:T(8,128)(2,1)}) %reduce-scatter.5.cloned.1.call-update) | async-done | bytes 262160 | tf_op jit(solution)/shard_map/reduce_scatter | solution.py:158
  302.8 1.0 convert_element_type.102
  303.8 4.9 %fusion.13 = bf16[64,4,2048]{2,1,0:T(4,128)(2,1)} fusion(bf16[64,4,2048]{2,1,0:T(4,128)(2,1)} %bitcast.149, f32[64,2048]{1,0:T(8,128)S(1)} %convert_element_type.102, f32[4]{0:T(128)S(1)} %get-tuple-element.21, pred[64]{0:T(512)(128)(4,1)S(1)} %lt.43, f32[2,4,4]{2,1,0:T(4,128)S(1)} %copy-done.12), kind=kOutput, calls=%fused_computation.21 | convolution fusion | flops 27262976 | bytes 2624512 | tf_op jit(solution)/shard_map/nkd,km->nmd/dot_general | solution.py:164
  (81 shorter events, 8.6 us)
Async XLA Ops:
  7.2 43.7 %copy-start = (bf16[512,2048]{1,0:T(8,128)(2,1)S(1)}, bf16[512,2048]{1,0:T(8,128)(2,1)}, u32[]{:S(2)}) copy-start(bf16[512,2048]{1,0:T(8,128)(2,1)} %param.22) | copy-start | bytes 6291460
  7.2 6.3 %copy-start.13 = (f32[2,4]{1,0:T(2,128)S(1)}, f32[2,4]{1,0:T(2,128)}, u32[]{:S(2)}) copy-start(f32[2,4]{1,0:T(2,128)} %param.28) | copy-start | bytes 100
  7.2 71.6 %reduce-scatter.3.cloned.1.call-start = ((), (), s32[]{:S(2)}) async-start(), calls=%async_computation.3 | async-start | bytes 1310720 | tf_op jit(solution)/shard_map/reduce_scatter | solution.py:131
  9.6 3.0 copy-start.6
  23.2 1.6 copy-start.9
  24.0 7.3 %copy-start.3 = (bf16[4,64,2048]{2,1,0:T(8,128)(2,1)}, bf16[4,64,2048]{2,1,0:T(8,128)(2,1)S(1)}, u32[]{:S(2)}) copy-start(bf16[4,64,2048]{2,1,0:T(8,128)(2,1)S(1)} %multiply_convert_fusion) | copy-start | bytes 3145732
  46.7 2.2 copy-start.8
  48.9 1.7 copy-start.4
  50.9 1.8 copy-start.5
  50.9 28.9 %copy-start.12 = (f32[2,4,4]{2,1,0:T(4,128)S(1)}, f32[2,4,4]{2,1,0:T(4,128)}, u32[]{:S(2)}) copy-start(f32[2,4,4]{2,1,0:T(4,128)} %param.29) | copy-start | bytes 388
  52.6 250.2 %reduce-scatter.5.cloned.1.call-start = ((), (), s32[]{:S(2)}) async-start(), calls=%async_computation.4 | async-start | bytes 8650752 | tf_op jit(solution)/shard_map/reduce_scatter | solution.py:158
  52.7 30.5 %copy-start.14 = (f32[2,4]{1,0:T(2,128)S(1)}, f32[2,4]{1,0:T(2,128)}, u32[]{:S(2)}) copy-start(f32[2,4]{1,0:T(2,128)} %param.28) | copy-start | bytes 100
  83.2 2.3 copy-start.15
  86.9 105.8 %copy-start.10 = (bf16[2048,256]{1,0:T(8,128)(2,1)S(1)}, bf16[2048,256]{1,0:T(8,128)(2,1)}, u32[]{:S(2)}) copy-start(bf16[2048,256]{1,0:T(8,128)(2,1)} %param.23) | copy-start | bytes 3145732
  189.4 3.2 %copy-start.2 = (bf16[32,64,2048]{2,1,0:T(8,128)(2,1)}, bf16[32,64,2048]{2,1,0:T(8,128)(2,1)S(1)}, u32[]{:S(2)}) copy-start(bf16[32,64,2048]{2,1,0:T(8,128)(2,1)S(1)} %all_to_all.5) | copy-start | bytes 25165828
  192.6 3.8 %copy-start.11 = (bf16[256,2048]{1,0:T(8,128)(2,1)S(1)}, bf16[256,2048]{1,0:T(8,128)(2,1)}, u32[]{:S(2)}) copy-start(bf16[256,2048]{1,0:T(8,128)(2,1)} %param.25) | copy-start | bytes 3145732
  213.3 0.6 copy-start.7
  303.8 5.0 %copy-start.1 = (bf16[512,2048]{1,0:T(8,128)(2,1)S(1)}, bf16[512,2048]{1,0:T(8,128)(2,1)}, u32[]{:S(2)}) copy-start(bf16[512,2048]{1,0:T(8,128)(2,1)} %param.22) | copy-start | bytes 6291460
Sparse Core Ops, SparseCore 0:
  52.8 26.0 reduce-scatter.2
  213.4 89.3 reduce-scatter.4
